TPU v7x, 256 devices: a whole 4x4x8 slice. The times are simulated.
256 devices in a mesh: dp: 32 (over y_lo, z, core), tensor: 8 (over y_hi, x).
Axes of the slice: x: 4, y: 4 (y_hi: 2, y_lo: 2; y = y_hi * 2 + y_lo), z: 8, core: 2. Of those that a mesh axis runs over, the one named last changes fastest.
Arguments:
- activations: bfloat16 [1024, 16384], P('dp', 'tensor'), may hold values from -6 to 6
- weight: bfloat16 [16384, 16384], P('tensor', 'dp'), may hold values from -0.046875 to 0.046875
- out_grad: bfloat16 [1024, 16384], P('tensor', 'dp'), may hold values from -6 to 6
Outputs:
- outputs: bfloat16 [1024, 16384], P('tensor', 'dp')
- in_grad: bfloat16 [1024, 16384], P('dp', 'tensor')
- weight_grad: float32 [16384, 16384], P('tensor', 'dp')
All inputs are finite; a program needn't handle non-finite values.
Results may differ from a plain program's by a relative error of at most 0.0049.
Values may be sent and summed in bfloat16 or wider, within the bound.
A program may use at most 64 MiB of HBM per device.

v0:
```python
import math
import jax
import jax.numpy as jnp
from jax import lax
from jax.sharding import PartitionSpec as P


def from_partner(shard, axis, apart):
    return lax.ppermute(shard, axis, [(i, i ^ 1 << apart) for i in range(lax.axis_size(axis))])


def signs_table(width):
    position = jnp.arange(width, dtype=jnp.int32)
    joined = jnp.bitwise_and(position[:, None], position[None, :])
    parity = jnp.zeros_like(joined)
    for bit_number in range(width.bit_length() - 1):
        parity = parity + jnp.bitwise_and(jnp.right_shift(joined, bit_number), 1)
    return jnp.where(parity % 2 == 1, -1.0, 1.0).astype(jnp.float32)


def transform(values, width):
    bit_count = width.bit_length() - 1
    first_size = 2 ** (bit_count // 2)
    second = width // first_size
    shaped = values.reshape(values.shape[0], first_size, second)
    result = jnp.einsum(
        "rab,ac->rcb", shaped, signs_table(first_size), precision=lax.Precision.HIGHEST
    )
    result = jnp.einsum("rcb,bd->rcd", result, signs_table(second), precision=lax.Precision.HIGHEST)
    return result.reshape(values.shape[0], width)


def rotate_pairs(values, width):
    result = transform(values, width)
    position = lax.axis_index("tensor")
    for bit_number in range(lax.axis_size("tensor").bit_length() - 1):
        other = from_partner(result, "tensor", bit_number)
        upper = jnp.bitwise_and(jnp.right_shift(position, bit_number), 1) == 1
        result = jnp.where(upper, other - result, result + other)
    return result


def per_device(activations, weight, out_grad):
    tensor_size = lax.axis_size("tensor")
    local_width = activations.shape[1]
    full_width = local_width * tensor_size
    factor = 1.0 / math.sqrt(full_width)
    grad_count = out_grad.shape[0]
    token_total = grad_count * tensor_size
    rotated = (rotate_pairs(activations.astype(jnp.float32), local_width) * factor).astype(
        jnp.bfloat16
    )
    grad_all = lax.all_gather(out_grad, "tensor", axis=0, tiled=True)
    rows_all = lax.all_gather(rotated, "dp", axis=0, tiled=True)
    weight_grad = lax.dot_general(
        rows_all, grad_all, (((0,), (0,)), ((), ())), preferred_element_type=jnp.float32
    )
    outputs = lax.psum_scatter(
        jnp.dot(rows_all, weight, preferred_element_type=jnp.float32),
        "tensor",
        scatter_dimension=0,
        tiled=True,
    ).astype(jnp.bfloat16)
    weight_grad = weight_grad * (1.0 / math.sqrt(token_total))
    rotated_grad = lax.psum_scatter(
        lax.dot_general(
            grad_all, weight, (((1,), (1,)), ((), ())), preferred_element_type=jnp.float32
        ),
        "dp",
        scatter_dimension=0,
        tiled=True,
    )
    in_grad = (rotate_pairs(rotated_grad, local_width) * factor).astype(jnp.bfloat16)
    return (outputs, in_grad, weight_grad)


def solution(mesh):
    return jax.shard_map(
        per_device,
        mesh=mesh,
        in_specs=(P("dp", "tensor"), P("tensor", "dp"), P("tensor", "dp")),
        out_specs=(P("tensor", "dp"), P("dp", "tensor"), P("tensor", "dp")),
        check_vma=False,
    )
```

profile of v0, /device:TPU:2, one launch (start us, length us, event | category | flops | bytes accessed | tf_op | source)
XLA Modules:
  0.0 356.3 jit_solution(6116350609848868271)
XLA Ops:
  7.2 0.0 copy-start
  7.2 0.0 all-gather.5.cloned.1.call-start
  7.2 1.3 reshape.18
  8.5 0.4 convolution_bitcast_fusion.1
  9.0 0.6 fusion.4
  9.6 0.2 reshape.19
  9.8 2.3 collective-permute-start
  12.1 0.0 all-gather.5.cloned.1.call-update
  12.2 0.0 all-gather.3.cloned.1.call-start
  12.2 5.7 %collective-permute-done = f32[32,2048]{1,0:T(8,128)S(1)} collective-permute-done((f32[32,2048]{1,0:T(8,128)S(1)}, f32[32,2048]{1,0:T(8,128)S(1)}, u32[]{:S(2)}, u32[]{:S(2)}) %collective-permute-start) | collective-permute-done | bytes 262176 | tf_op jit(solution)/shard_map/ppermute | solution.py:9
  17.9 2.2 collective-permute-start.1
  20.1 6.3 %collective-permute-done.1 = f32[32,2048]{1,0:T(8,128)S(1)} collective-permute-done((f32[32,2048]{1,0:T(8,128)S(1)}, f32[32,2048]{1,0:T(8,128)S(1)}, u32[]{:S(2)}, u32[]{:S(2)}) %collective-permute-start.1) | collective-permute-done | bytes 262176 | tf_op jit(solution)/shard_map/ppermute | solution.py:9
  26.4 3.6 %collective-permute-start.2 = (f32[32,2048]{1,0:T(8,128)S(1)}, f32[32,2048]{1,0:T(8,128)S(1)}, u32[]{:S(2)}, u32[]{:S(2)}) collective-permute-start(f32[32,2048]{1,0:T(8,128)S(1)} %add_select_fusion.2), channel_id=1, source_target_pairs={{0,4},{1,5},{2,6},{3,7},{4,0},{5,1},{6,2},{7,3},{8,12},{9,13},{10,... | collective-permute-start | bytes 786440 | tf_op jit(solution)/shard_map/ppermute | solution.py:9
  30.0 5.9 %collective-permute-done.2 = f32[32,2048]{1,0:T(8,128)S(1)} collective-permute-done((f32[32,2048]{1,0:T(8,128)S(1)}, f32[32,2048]{1,0:T(8,128)S(1)}, u32[]{:S(2)}, u32[]{:S(2)}) %collective-permute-start.2) | collective-permute-done | bytes 262176 | tf_op jit(solution)/shard_map/ppermute | solution.py:9
  35.9 0.7 multiply_convert_fusion.1
  36.6 0.0 all-gather.3.cloned.1.call-update
  36.6 0.0 reduce-scatter.5.cloned.1.call-start
  36.7 29.8 %all-gather.5.cloned.1.call-done = bf16[1024,512]{1,0:T(8,128)(2,1)} async-done(((bf16[128,512]{1,0:T(8,128)(2,1)}), bf16[1024,512]{1,0:T(8,128)(2,1)}) %all-gather.5.cloned.1.call-update) | async-done | bytes 1048592 | tf_op jit(solution)/shard_map/all_gather | solution.py:53
  66.4 0.0 copy-done
  66.4 6.8 %fusion.57 = f32[1024,2048]{1,0:T(8,128)} fusion(bf16[1024,512]{1,0:T(8,128)(2,1)} %all-gather.5.cloned.1.call-done, bf16[2048,512]{1,0:T(8,128)(2,1)S(1)} %copy-done), kind=kOutput, calls=%fused_computation.68 | convolution fusion | flops 2147483648 | bytes 11534336 | tf_op jit(solution)/shard_map/dot_general | solution.py:66
  73.3 0.0 reduce-scatter.5.cloned.1.call-update
  73.3 0.0 reduce-scatter.3.cloned.1.call-start
  73.3 61.5 %all-gather.3.cloned.1.call-done = bf16[1024,2048]{1,0:T(8,128)(2,1)} async-done(((bf16[32,2048]{1,0:T(8,128)(2,1)}), bf16[1024,2048]{1,0:T(8,128)(2,1)}) %all-gather.3.cloned.1.call-update) | async-done | bytes 4194320 | tf_op jit(solution)/shard_map/all_gather | solution.py:54
  134.9 5.8 %fusion.56 = f32[1024,512]{1,0:T(8,128)} fusion(bf16[1024,2048]{1,0:T(8,128)(2,1)} %all-gather.3.cloned.1.call-done, bf16[2048,512]{1,0:T(8,128)(2,1)S(1)} %copy-done), kind=kOutput, calls=%fused_computation.67 | convolution fusion | flops 2147483648 | bytes 8388608 | tf_op jit(solution)/shard_map/dot_general | solution.py:59
  140.7 0.0 reduce-scatter.3.cloned.1.call-update
  140.7 125.6 %reduce-scatter.5.cloned.1.call-done = f32[32,2048]{1,0:T(8,128)} async-done(((f32[1024,2048]{1,0:T(8,128)}), f32[32,2048]{1,0:T(8,128)}) %reduce-scatter.5.cloned.1.call-update) | async-done | bytes 262160 | tf_op jit(solution)/shard_map/reduce_scatter | solution.py:65
  266.4 1.1 reshape.20
  267.5 0.6 convolution_bitcast_fusion
  268.2 0.6 fusion.2
  268.8 0.2 reshape.21
  268.9 0.2 collective-permute-start.3
  269.2 7.7 %collective-permute-done.3 = f32[32,2048]{1,0:T(8,128)S(1)} collective-permute-done((f32[32,2048]{1,0:T(8,128)S(1)}, f32[32,2048]{1,0:T(8,128)S(1)}, u32[]{:S(2)}, u32[]{:S(2)}) %collective-permute-start.3) | collective-permute-done | bytes 262176 | tf_op jit(solution)/shard_map/ppermute | solution.py:9
  276.9 2.9 collective-permute-start.4
  279.7 5.2 %collective-permute-done.4 = f32[32,2048]{1,0:T(8,128)S(1)} collective-permute-done((f32[32,2048]{1,0:T(8,128)S(1)}, f32[32,2048]{1,0:T(8,128)S(1)}, u32[]{:S(2)}, u32[]{:S(2)}) %collective-permute-start.4) | collective-permute-done | bytes 262176 | tf_op jit(solution)/shard_map/ppermute | solution.py:9
  284.9 4.0 %collective-permute-start.5 = (f32[32,2048]{1,0:T(8,128)S(1)}, f32[32,2048]{1,0:T(8,128)S(1)}, u32[]{:S(2)}, u32[]{:S(2)}) collective-permute-start(f32[32,2048]{1,0:T(8,128)S(1)} %add_select_fusion), channel_id=1, source_target_pairs={{0,4},{1,5},{2,6},{3,7},{4,0},{5,1},{6,2},{7,3},{8,12},{9,13},{10,... | collective-permute-start | bytes 786440 | tf_op jit(solution)/shard_map/ppermute | solution.py:9
  289.0 6.9 %convolution_multiply_fusion = f32[2048,512]{1,0:T(8,128)} fusion(bf16[1024,2048]{1,0:T(8,128)(2,1)} %all-gather.3.cloned.1.call-done, bf16[1024,512]{1,0:T(8,128)(2,1)} %all-gather.5.cloned.1.call-done), kind=kOutput, calls=%fused_computation | convolution fusion | flops 2148532224 | bytes 9437184 | tf_op jit(solution)/shard_map/dot_general | solution.py:55
  295.9 51.6 %reduce-scatter.3.cloned.1.call-done = f32[128,512]{1,0:T(8,128)} async-done(((f32[1024,512]{1,0:T(8,128)}), f32[128,512]{1,0:T(8,128)}) %reduce-scatter.3.cloned.1.call-update) | async-done | bytes 262160 | tf_op jit(solution)/shard_map/reduce_scatter | solution.py:58
  347.5 1.6 convert_element_type.11
  349.1 0.0 collective-permute-done.5
  349.1 0.7 multiply_convert_fusion
  (4 shorter events, 0.1 us)
Async XLA Ops:
  7.2 59.3 %copy-start = (bf16[2048,512]{1,0:T(8,128)(2,1)S(1)}, bf16[2048,512]{1,0:T(8,128)(2,1)}, u32[]{:S(2)}) copy-start(bf16[2048,512]{1,0:T(8,128)(2,1)} %param.4) | copy-start | bytes 6291460
  7.2 59.3 %all-gather.5.cloned.1.call-start = ((), (), s32[]{:S(2)}) async-start(), calls=%async_computation.4 | async-start | bytes 1179648 | tf_op jit(solution)/shard_map/all_gather | solution.py:53
  9.8 8.1 %collective-permute-start = (f32[32,2048]{1,0:T(8,128)S(1)}, f32[32,2048]{1,0:T(8,128)S(1)}, u32[]{:S(2)}, u32[]{:S(2)}) collective-permute-start(f32[32,2048]{1,0:T(8,128)S(1)} %reshape.19), channel_id=1, source_target_pairs={{0,1},{1,0},{2,3},{3,2},{4,5},{5,4},{6,7},{7,6},{8,9},{9,8},{10,11... | collective-permute-start | bytes 786440 | tf_op jit(solution)/shard_map/ppermute | solution.py:9
  12.2 122.7 %all-gather.3.cloned.1.call-start = ((), (), s32[]{:S(2)}) async-start(), calls=%async_computation.2 | async-start | bytes 4325376 | tf_op jit(solution)/shard_map/all_gather | solution.py:54
  17.9 8.5 %collective-permute-start.1 = (f32[32,2048]{1,0:T(8,128)S(1)}, f32[32,2048]{1,0:T(8,128)S(1)}, u32[]{:S(2)}, u32[]{:S(2)}) collective-permute-start(f32[32,2048]{1,0:T(8,128)S(1)} %add_select_fusion.3), channel_id=1, source_target_pairs={{0,2},{1,3},{2,0},{3,1},{4,6},{5,7},{6,4},{7,5},{8,10},{9,11},{10,... | collective-permute-start | bytes 786440 | tf_op jit(solution)/shard_map/ppermute | solution.py:9
  26.4 9.5 %collective-permute-start.2 = (f32[32,2048]{1,0:T(8,128)S(1)}, f32[32,2048]{1,0:T(8,128)S(1)}, u32[]{:S(2)}, u32[]{:S(2)}) collective-permute-start(f32[32,2048]{1,0:T(8,128)S(1)} %add_select_fusion.2), channel_id=1, source_target_pairs={{0,4},{1,5},{2,6},{3,7},{4,0},{5,1},{6,2},{7,3},{8,12},{9,13},{10,... | collective-permute-start | bytes 786440 | tf_op jit(solution)/shard_map/ppermute | solution.py:9
  36.6 229.7 %reduce-scatter.5.cloned.1.call-start = ((), (), s32[]{:S(2)}) async-start(), calls=%async_computation.5 | async-start | bytes 8650752 | tf_op jit(solution)/shard_map/reduce_scatter | solution.py:65
  73.3 274.2 %reduce-scatter.3.cloned.1.call-start = ((), (), s32[]{:S(2)}) async-start(), calls=%async_computation.3 | async-start | bytes 2359296 | tf_op jit(solution)/shard_map/reduce_scatter | solution.py:58
  268.9 7.9 %collective-permute-start.3 = (f32[32,2048]{1,0:T(8,128)S(1)}, f32[32,2048]{1,0:T(8,128)S(1)}, u32[]{:S(2)}, u32[]{:S(2)}) collective-permute-start(f32[32,2048]{1,0:T(8,128)S(1)} %reshape.21), channel_id=1, source_target_pairs={{0,1},{1,0},{2,3},{3,2},{4,5},{5,4},{6,7},{7,6},{8,9},{9,8},{10,11... | collective-permute-start | bytes 786440 | tf_op jit(solution)/shard_map/ppermute | solution.py:9
  276.9 8.0 %collective-permute-start.4 = (f32[32,2048]{1,0:T(8,128)S(1)}, f32[32,2048]{1,0:T(8,128)S(1)}, u32[]{:S(2)}, u32[]{:S(2)}) collective-permute-start(f32[32,2048]{1,0:T(8,128)S(1)} %add_select_fusion.1), channel_id=1, source_target_pairs={{0,2},{1,3},{2,0},{3,1},{4,6},{5,7},{6,4},{7,5},{8,10},{9,11},{10,... | collective-permute-start | bytes 786440 | tf_op jit(solution)/shard_map/ppermute | solution.py:9
  284.9 64.2 %collective-permute-start.5 = (f32[32,2048]{1,0:T(8,128)S(1)}, f32[32,2048]{1,0:T(8,128)S(1)}, u32[]{:S(2)}, u32[]{:S(2)}) collective-permute-start(f32[32,2048]{1,0:T(8,128)S(1)} %add_select_fusion), channel_id=1, source_target_pairs={{0,4},{1,5},{2,6},{3,7},{4,0},{5,1},{6,2},{7,3},{8,12},{9,13},{10,... | collective-permute-start | bytes 786440 | tf_op jit(solution)/shard_map/ppermute | solution.py:9
Sparse Core Ops, SparseCore 0:
  12.3 54.1 all-gather.4
  68.9 65.9 all-gather.2
  137.4 128.8 reduce-scatter.4
  270.3 77.1 reduce-scatter.2
where the time goes:
time: 357 us; the launch traced here: 356 us
  waiting for transfers between devices  299 us (84%)
  matrix products  21.9 us (6%)
  starting transfers between devices  15.4 us (4%)
  between operations  13.8 us (4%)
    reduce_scatter x1, waiting for transfers between devices, per_device(): lax.psum_scatter(lax.dot_general(grad_all, weight, (((1,), (1,)), ((), ()...  126 us
    all_gather x1, waiting for transfers between devices, per_device(): rows_all = lax.all_gather(rotated, 'dp', axis=0, tiled=True)  61.5 us
    reduce_scatter x1, waiting for transfers between devices, per_device(): lax.psum_scatter(jnp.dot(rows_all, weight, preferred_element_type=jnp.flo...  51.6 us
    ppermute x6, waiting for transfers between devices, from_partner(): lax.ppermute(shard, axis, [(i, i ^ 1 << apart) for i in range(lax.axis_si...  30.7 us
    all_gather x1, waiting for transfers between devices, per_device(): grad_all = lax.all_gather(out_grad, 'tensor', axis=0, tiled=True)  29.8 us
    ppermute x6, starting transfers between devices, from_partner(): lax.ppermute(shard, axis, [(i, i ^ 1 << apart) for i in range(lax.axis_si...  15.2 us
  transfers between devices with their start and end apart: 10, of which 9 were waited for; matrix products, arithmetic and copies ran while one was open for 7% of the time, Pallas kernels for 0%

commit v1 on v0

--- a/solution.py
+++ b/solution.py
@@ -50,7 +50,9 @@
     rotated = (rotate_pairs(activations.astype(jnp.float32), local_width) * factor).astype(
         jnp.bfloat16
     )
-    grad_all = lax.all_gather(out_grad, "tensor", axis=0, tiled=True)
+    grad_all = jnp.concatenate(
+        lax.all_to_all(jnp.stack([out_grad] * lax.axis_size("tensor")), "tensor", 0, 0), axis=0
+    )
     rows_all = lax.all_gather(rotated, "dp", axis=0, tiled=True)
     weight_grad = lax.dot_general(
         rows_all, grad_all, (((0,), (0,)), ((), ())), preferred_element_type=jnp.float32

time: 357 us -> 328 us (0.919)
  waiting for transfers between devices: 299 us -> 248 us
  blocking collectives: 0 us -> 20.7 us
    all_gather x1 -> x0, waiting for transfers between devices: 29.8 us -> none  [per_device(): grad_all = lax.all_gather(out_grad, 'tensor', axis=0, tiled=True)]
    all_to_all x0 -> x1, blocking collectives: none -> 20.7 us  [per_device(): lax.all_to_all(jnp.stack([out_grad] * lax.axis_size('tensor')), 'tensor',...]
    all_gather x1, waiting for transfers between devices: 61.5 us -> 42.9 us  [per_device(): rows_all = lax.all_gather(rotated, 'dp', axis=0, tiled=True)]
  transfers between devices with their start and end apart: 10 -> 9, of which waited for: 9 -> 8; matrix products, arithmetic and copies ran while one was open for 7% -> 7% of each run, Pallas kernels for 0% -> 0%
where the time goes in v1:
time: 328 us
  waiting for transfers between devices  248 us (76%)
  blocking collectives  20.7 us (6%)
  matrix products  20.6 us (6%)
  starting transfers between devices  17.1 us (5%)
  between operations  13.8 us (4%)
  local copies, waits for them, and re-layouts  3.93 us (1%)
    reduce_scatter x1, waiting for transfers between devices, per_device(): lax.psum_scatter(lax.dot_general(grad_all, weight, (((1,), (1,)), ((), ()...  126 us
    reduce_scatter x1, waiting for transfers between devices, per_device(): lax.psum_scatter(jnp.dot(rows_all, weight, preferred_element_type=jnp.flo...  51.8 us
    all_gather x1, waiting for transfers between devices, per_device(): rows_all = lax.all_gather(rotated, 'dp', axis=0, tiled=True)  42.9 us
    ppermute x6, waiting for transfers between devices, from_partner(): lax.ppermute(shard, axis, [(i, i ^ 1 << apart) for i in range(lax.axis_si...  27.9 us
    all_to_all x1, blocking collectives, per_device(): lax.all_to_all(jnp.stack([out_grad] * lax.axis_size('tensor')), 'tensor',...  20.7 us
    ppermute x6, starting transfers between devices, from_partner(): lax.ppermute(shard, axis, [(i, i ^ 1 << apart) for i in range(lax.axis_si...  17 us
    dot_general x1, matrix products, per_device(): lax.dot_general(rows_all, grad_all, (((0,), (0,)), ((), ())), preferred_e...  6.96 us
  transfers between devices with their start and end apart: 9, of which 8 were waited for; matrix products, arithmetic and copies ran while one was open for 7% of the time, Pallas kernels for 0%

profile of v1, /device:TPU:2, one launch (start us, length us, event | category | flops | bytes accessed | tf_op | source)
XLA Modules:
  0.0 327.6 jit_solution(3059029615582599693)
XLA Ops:
  7.2 0.0 copy-start
  7.2 0.0 copy-start.2
  7.2 0.0 all-gather.2.cloned.1.call-start
  7.2 1.3 reshape.23
  8.6 0.4 convolution_bitcast_fusion.1
  9.0 0.6 fusion.4
  9.6 0.2 reshape.24
  9.8 2.4 collective-permute-start
  12.2 5.8 %collective-permute-done = f32[32,2048]{1,0:T(8,128)S(1)} collective-permute-done((f32[32,2048]{1,0:T(8,128)S(1)}, f32[32,2048]{1,0:T(8,128)S(1)}, u32[]{:S(2)}, u32[]{:S(2)}) %collective-permute-start) | collective-permute-done | bytes 262176 | tf_op jit(solution)/shard_map/ppermute | solution.py:9
  18.0 2.2 collective-permute-start.1
  20.2 6.3 %collective-permute-done.1 = f32[32,2048]{1,0:T(8,128)S(1)} collective-permute-done((f32[32,2048]{1,0:T(8,128)S(1)}, f32[32,2048]{1,0:T(8,128)S(1)}, u32[]{:S(2)}, u32[]{:S(2)}) %collective-permute-start.1) | collective-permute-done | bytes 262176 | tf_op jit(solution)/shard_map/ppermute | solution.py:9
  26.5 3.6 %collective-permute-start.2 = (f32[32,2048]{1,0:T(8,128)S(1)}, f32[32,2048]{1,0:T(8,128)S(1)}, u32[]{:S(2)}, u32[]{:S(2)}) collective-permute-start(f32[32,2048]{1,0:T(8,128)S(1)} %add_select_fusion.2), channel_id=1, source_target_pairs={{0,4},{1,5},{2,6},{3,7},{4,0},{5,1},{6,2},{7,3},{8,12},{9,13},{10,... | collective-permute-start | bytes 786440 | tf_op jit(solution)/shard_map/ppermute | solution.py:9
  30.0 4.5 %collective-permute-done.2 = f32[32,2048]{1,0:T(8,128)S(1)} collective-permute-done((f32[32,2048]{1,0:T(8,128)S(1)}, f32[32,2048]{1,0:T(8,128)S(1)}, u32[]{:S(2)}, u32[]{:S(2)}) %collective-permute-start.2) | collective-permute-done | bytes 262176 | tf_op jit(solution)/shard_map/ppermute | solution.py:9
  34.6 0.7 multiply_convert_fusion.1
  35.3 0.0 all-gather.2.cloned.1.call-update
  35.3 0.0 reduce-scatter.5.cloned.1.call-start
  35.3 0.0 copy-done.2
  35.3 0.1 stack.2
  35.4 20.7 %all_to_all.5 = bf16[8,128,512]{2,1,0:T(8,128)(2,1)S(1)} all-to-all(bf16[8,128,512]{2,1,0:T(8,128)(2,1)S(1)} %stack.2), channel_id=1, replica_groups=mesh['dp'=32,'tensor'=8] {'tensor'}, dimensions={0} | all-to-all | bytes 2097152 | tf_op jit(solution)/shard_map/all_to_all | solution.py:54
  56.1 0.0 copy-start.1
  56.1 1.0 copy-done.1
  57.1 0.0 copy-done
  57.1 5.6 %fusion.57 = f32[1024,2048]{1,0:T(8,128)} fusion(bf16[1024,512]{1,0:T(8,128)(2,1)S(1)} %bitcast.25, bf16[2048,512]{1,0:T(8,128)(2,1)S(1)} %copy-done), kind=kOutput, calls=%fused_computation.68 | convolution fusion | flops 2147483648 | bytes 11534336 | tf_op jit(solution)/shard_map/dot_general | solution.py:68
  62.7 0.0 reduce-scatter.5.cloned.1.call-update
  62.7 0.0 reduce-scatter.3.cloned.1.call-start
  62.8 42.9 %all-gather.2.cloned.1.call-done = bf16[1024,2048]{1,0:T(8,128)(2,1)} async-done(((bf16[32,2048]{1,0:T(8,128)(2,1)}), bf16[1024,2048]{1,0:T(8,128)(2,1)}) %all-gather.2.cloned.1.call-update) | async-done | bytes 4194320 | tf_op jit(solution)/shard_map/all_gather | solution.py:56
  105.6 5.8 %fusion.56 = f32[1024,512]{1,0:T(8,128)} fusion(bf16[1024,2048]{1,0:T(8,128)(2,1)} %all-gather.2.cloned.1.call-done, bf16[2048,512]{1,0:T(8,128)(2,1)S(1)} %copy-done), kind=kOutput, calls=%fused_computation.67 | convolution fusion | flops 2147483648 | bytes 8388608 | tf_op jit(solution)/shard_map/dot_general | solution.py:61
  111.4 0.0 reduce-scatter.3.cloned.1.call-update
  111.5 125.6 %reduce-scatter.5.cloned.1.call-done = f32[32,2048]{1,0:T(8,128)} async-done(((f32[1024,2048]{1,0:T(8,128)}), f32[32,2048]{1,0:T(8,128)}) %reduce-scatter.5.cloned.1.call-update) | async-done | bytes 262160 | tf_op jit(solution)/shard_map/reduce_scatter | solution.py:67
  237.1 1.1 reshape.26
  238.3 0.6 convolution_bitcast_fusion
  238.9 0.6 fusion.2
  239.5 0.2 reshape.27
  239.7 1.0 collective-permute-start.3
  240.7 6.5 %collective-permute-done.3 = f32[32,2048]{1,0:T(8,128)S(1)} collective-permute-done((f32[32,2048]{1,0:T(8,128)S(1)}, f32[32,2048]{1,0:T(8,128)S(1)}, u32[]{:S(2)}, u32[]{:S(2)}) %collective-permute-start.3) | collective-permute-done | bytes 262176 | tf_op jit(solution)/shard_map/ppermute | solution.py:9
  247.2 3.9 %collective-permute-start.4 = (f32[32,2048]{1,0:T(8,128)S(1)}, f32[32,2048]{1,0:T(8,128)S(1)}, u32[]{:S(2)}, u32[]{:S(2)}) collective-permute-start(f32[32,2048]{1,0:T(8,128)S(1)} %add_select_fusion.1), channel_id=1, source_target_pairs={{0,2},{1,3},{2,0},{3,1},{4,6},{5,7},{6,4},{7,5},{8,10},{9,11},{10,... | collective-permute-start | bytes 786440 | tf_op jit(solution)/shard_map/ppermute | solution.py:9
  251.1 4.8 %collective-permute-done.4 = f32[32,2048]{1,0:T(8,128)S(1)} collective-permute-done((f32[32,2048]{1,0:T(8,128)S(1)}, f32[32,2048]{1,0:T(8,128)S(1)}, u32[]{:S(2)}, u32[]{:S(2)}) %collective-permute-start.4) | collective-permute-done | bytes 262176 | tf_op jit(solution)/shard_map/ppermute | solution.py:9
  256.0 4.0 %collective-permute-start.5 = (f32[32,2048]{1,0:T(8,128)S(1)}, f32[32,2048]{1,0:T(8,128)S(1)}, u32[]{:S(2)}, u32[]{:S(2)}) collective-permute-start(f32[32,2048]{1,0:T(8,128)S(1)} %add_select_fusion), channel_id=1, source_target_pairs={{0,4},{1,5},{2,6},{3,7},{4,0},{5,1},{6,2},{7,3},{8,12},{9,13},{10,... | collective-permute-start | bytes 786440 | tf_op jit(solution)/shard_map/ppermute | solution.py:9
  260.0 7.0 %convolution_multiply_fusion = f32[2048,512]{1,0:T(8,128)} fusion(bf16[1024,2048]{1,0:T(8,128)(2,1)} %all-gather.2.cloned.1.call-done, bf16[1024,512]{1,0:T(8,128)(2,1)} %bitcast.26), kind=kOutput, calls=%fused_computation | convolution fusion | flops 2148532224 | bytes 9437184 | tf_op jit(solution)/shard_map/dot_general | solution.py:57
  266.9 51.8 %reduce-scatter.3.cloned.1.call-done = f32[128,512]{1,0:T(8,128)} async-done(((f32[1024,512]{1,0:T(8,128)}), f32[128,512]{1,0:T(8,128)}) %reduce-scatter.3.cloned.1.call-update) | async-done | bytes 262160 | tf_op jit(solution)/shard_map/reduce_scatter | solution.py:60
  318.7 1.6 convert_element_type.11
  320.4 0.0 collective-permute-done.5
  320.4 0.7 multiply_convert_fusion
  (4 shorter events, 0.1 us)
Async XLA Ops:
  7.2 49.9 %copy-start = (bf16[2048,512]{1,0:T(8,128)(2,1)S(1)}, bf16[2048,512]{1,0:T(8,128)(2,1)}, u32[]{:S(2)}) copy-start(bf16[2048,512]{1,0:T(8,128)(2,1)} %param.4) | copy-start | bytes 6291460
  7.2 28.1 %copy-start.2 = (bf16[128,512]{1,0:T(8,128)(2,1)S(1)}, bf16[128,512]{1,0:T(8,128)(2,1)}, u32[]{:S(2)}) copy-start(bf16[128,512]{1,0:T(8,128)(2,1)} %param.5) | copy-start | bytes 393220
  7.2 98.4 %all-gather.2.cloned.1.call-start = ((), (), s32[]{:S(2)}) async-start(), calls=%async_computation.3 | async-start | bytes 4325376 | tf_op jit(solution)/shard_map/all_gather | solution.py:56
  9.8 8.1 %collective-permute-start = (f32[32,2048]{1,0:T(8,128)S(1)}, f32[32,2048]{1,0:T(8,128)S(1)}, u32[]{:S(2)}, u32[]{:S(2)}) collective-permute-start(f32[32,2048]{1,0:T(8,128)S(1)} %reshape.24), channel_id=1, source_target_pairs={{0,1},{1,0},{2,3},{3,2},{4,5},{5,4},{6,7},{7,6},{8,9},{9,8},{10,11... | collective-permute-start | bytes 786440 | tf_op jit(solution)/shard_map/ppermute | solution.py:9
  18.0 8.5 %collective-permute-start.1 = (f32[32,2048]{1,0:T(8,128)S(1)}, f32[32,2048]{1,0:T(8,128)S(1)}, u32[]{:S(2)}, u32[]{:S(2)}) collective-permute-start(f32[32,2048]{1,0:T(8,128)S(1)} %add_select_fusion.3), channel_id=1, source_target_pairs={{0,2},{1,3},{2,0},{3,1},{4,6},{5,7},{6,4},{7,5},{8,10},{9,11},{10,... | collective-permute-start | bytes 786440 | tf_op jit(solution)/shard_map/ppermute | solution.py:9
  26.5 8.1 %collective-permute-start.2 = (f32[32,2048]{1,0:T(8,128)S(1)}, f32[32,2048]{1,0:T(8,128)S(1)}, u32[]{:S(2)}, u32[]{:S(2)}) collective-permute-start(f32[32,2048]{1,0:T(8,128)S(1)} %add_select_fusion.2), channel_id=1, source_target_pairs={{0,4},{1,5},{2,6},{3,7},{4,0},{5,1},{6,2},{7,3},{8,12},{9,13},{10,... | collective-permute-start | bytes 786440 | tf_op jit(solution)/shard_map/ppermute | solution.py:9
  35.3 201.8 %reduce-scatter.5.cloned.1.call-start = ((), (), s32[]{:S(2)}) async-start(), calls=%async_computation.5 | async-start | bytes 8650752 | tf_op jit(solution)/shard_map/reduce_scatter | solution.py:67
  56.1 1.0 copy-start.1
  62.7 256.0 %reduce-scatter.3.cloned.1.call-start = ((), (), s32[]{:S(2)}) async-start(), calls=%async_computation.4 | async-start | bytes 2359296 | tf_op jit(solution)/shard_map/reduce_scatter | solution.py:60
  239.7 7.5 %collective-permute-start.3 = (f32[32,2048]{1,0:T(8,128)S(1)}, f32[32,2048]{1,0:T(8,128)S(1)}, u32[]{:S(2)}, u32[]{:S(2)}) collective-permute-start(f32[32,2048]{1,0:T(8,128)S(1)} %reshape.27), channel_id=1, source_target_pairs={{0,1},{1,0},{2,3},{3,2},{4,5},{5,4},{6,7},{7,6},{8,9},{9,8},{10,11... | collective-permute-start | bytes 786440 | tf_op jit(solution)/shard_map/ppermute | solution.py:9
  247.2 8.7 %collective-permute-start.4 = (f32[32,2048]{1,0:T(8,128)S(1)}, f32[32,2048]{1,0:T(8,128)S(1)}, u32[]{:S(2)}, u32[]{:S(2)}) collective-permute-start(f32[32,2048]{1,0:T(8,128)S(1)} %add_select_fusion.1), channel_id=1, source_target_pairs={{0,2},{1,3},{2,0},{3,1},{4,6},{5,7},{6,4},{7,5},{8,10},{9,11},{10,... | collective-permute-start | bytes 786440 | tf_op jit(solution)/shard_map/ppermute | solution.py:9
  256.0 64.4 %collective-permute-start.5 = (f32[32,2048]{1,0:T(8,128)S(1)}, f32[32,2048]{1,0:T(8,128)S(1)}, u32[]{:S(2)}, u32[]{:S(2)}) collective-permute-start(f32[32,2048]{1,0:T(8,128)S(1)} %add_select_fusion), channel_id=1, source_target_pairs={{0,4},{1,5},{2,6},{3,7},{4,0},{5,1},{6,2},{7,3},{8,12},{9,13},{10,... | collective-permute-start | bytes 786440 | tf_op jit(solution)/shard_map/ppermute | solution.py:9
Sparse Core Ops, SparseCore 0:
  35.4 70.1 all-gather.1
  108.2 128.8 reduce-scatter.4
  241.2 77.5 reduce-scatter.2
